TPU v7x, 256 devices: a whole 4x4x8 slice. The times are simulated.
256 devices in a mesh: fsdp: 32 (over y, x, core), rep: 8 (over z).
Axes of the slice: x: 4, y: 4, z: 8, core: 2. Of those that a mesh axis runs over, the one named last changes fastest.
Arguments:
- tokens: bfloat16 [8, 4096, 2048], P('rep', 'fsdp'), may hold values from -6 to 6
- upstream: bfloat16 [8, 7168, 4096], P('rep', 'fsdp'), may hold values from -0.25 to 0.25
- weight: bfloat16 [2, 7168, 2048], P(None, 'fsdp'), may hold values from -0.125 to 0.125
- feedback: float32 [8, 2, 7168, 2048], P('rep', None, 'fsdp'), may hold values from -6 to 6
- momentum: float32 [2, 7168, 2048], P(None, 'fsdp', 'rep'), may hold values from -6 to 6
- right_factor: float32 [2, 7168, 64], P(None, 'fsdp'), may hold values from -6 to 6
Outputs:
- feedback_next: float32 [8, 2, 7168, 2048], P('rep', None, 'fsdp')
- momentum_next: float32 [2, 7168, 2048], P(None, 'fsdp', 'rep')
- weight_next: bfloat16 [2, 7168, 2048], P(None, 'fsdp', 'rep')
- right_next: float32 [2, 7168, 64], P(None, 'fsdp')
All inputs are finite; a program needn't handle non-finite values.
Results may differ from a plain program's by a relative error of at most 0.0023.
Values may be sent and summed in bfloat16 or wider, within the bound.
A program may use at most 128 MiB of HBM per device.

v0:
```python
import jax
import jax.numpy as jnp
from jax import lax
from jax.sharding import PartitionSpec as P

momentum_decay = 0.9
step_rate = 0.05
highest = lax.Precision.HIGHEST


def silu_pair(gate_pre):
    sigmoid = jax.nn.sigmoid(gate_pre)
    return (gate_pre * sigmoid, sigmoid * (1.0 + gate_pre * (1.0 - sigmoid)))


def solve_basis(factor, gram_matrix):
    lower_factor = jnp.linalg.cholesky(gram_matrix)
    return lax.linalg.triangular_solve(
        lower_factor, factor, left_side=False, lower=True, transpose_a=True
    )


def local_gram(factor):
    return jnp.einsum("kdr,kds->krs", factor, factor, precision=highest)


def per_device(tokens, upstream, weight, feedback, momentum, right_factor):
    own_rows = tokens[0]
    cotangents = upstream[0]
    contract_last = (((1,), (1,)), ((), ()))
    segment = lax.all_gather(own_rows, "fsdp", axis=0, tiled=True)
    cotangent_wide = cotangents.astype(jnp.float32)
    gate_pre = lax.dot_general(
        weight[0], segment, contract_last, preferred_element_type=jnp.float32
    )
    up_pre = lax.dot_general(weight[1], segment, contract_last, preferred_element_type=jnp.float32)
    activated, derivative = silu_pair(gate_pre)
    grad_gate = (cotangent_wide * up_pre * derivative).astype(jnp.bfloat16)
    grad_up = (cotangent_wide * activated).astype(jnp.bfloat16)
    term_gate = jnp.dot(grad_gate, segment, preferred_element_type=jnp.float32)
    term_up = jnp.dot(grad_up, segment, preferred_element_type=jnp.float32)
    gradient = jnp.stack([term_gate, term_up])
    delta = gradient + feedback[0]
    left_part = jnp.einsum("kfd,kfr->kdr", delta, right_factor, precision=highest)
    replicas = lax.axis_size("rep")
    left_mean = lax.psum(left_part, ("fsdp", "rep")) / replicas
    basis = solve_basis(left_mean, local_gram(left_mean))
    right_part = jnp.einsum("kfd,kdr->kfr", delta, basis, precision=highest)
    right_next = lax.psum(right_part, "rep") / replicas
    approx = jnp.einsum("kdr,kfr->kfd", basis, right_next, precision=highest)
    feedback_next = (delta - approx)[None]
    slab_cols = momentum.shape[2]
    slab_start = lax.axis_index("rep") * slab_cols
    approx_slab = lax.dynamic_slice_in_dim(approx, slab_start, slab_cols, 2)
    weight_slab = lax.dynamic_slice_in_dim(weight, slab_start, slab_cols, 2)
    momentum_next = momentum_decay * momentum + approx_slab
    weight_next = (weight_slab.astype(jnp.float32) - step_rate * momentum_next).astype(jnp.bfloat16)
    return (feedback_next, momentum_next, weight_next, right_next)


def solution(mesh):
    placed = (
        P("rep", "fsdp", None),
        P("rep", "fsdp", None),
        P(None, "fsdp", None),
        P("rep", None, "fsdp", None),
        P(None, "fsdp", "rep"),
        P(None, "fsdp", None),
    )
    return jax.shard_map(
        per_device,
        mesh=mesh,
        in_specs=placed,
        out_specs=(
            P("rep", None, "fsdp", None),
            P(None, "fsdp", "rep"),
            P(None, "fsdp", "rep"),
            P(None, "fsdp", None),
        ),
        check_vma=False,
    )
```

profile of v0, /device:TPU:2, one launch (start us, length us, event | category | flops | bytes accessed | tf_op | source)
XLA Modules:
  0.0 520.9 jit_solution(15495969798062645339)
XLA Ops:
  7.2 0.0 all-gather.3.cloned.1.call-start
  7.2 0.7 all-gather.3.cloned.1.call-update
  7.9 0.0 all-reduce.3.cloned.1.call-start
  8.0 83.1 %all-gather.3.cloned.1.call-done = bf16[1,4096,2048]{2,1,0:T(8,128)(2,1)} async-done(((bf16[1,128,2048]{2,1,0:T(8,128)(2,1)}), bf16[1,4096,2048]{2,1,0:T(8,128)(2,1)}) %all-gather.3.cloned.1.call-update) | async-done | bytes 16777232 | tf_op jit(solution)/shard_map/all_gather | solution.py:31
  91.1 13.0 %fusion.4 = f32[224,4096]{1,0:T(8,128)} fusion(bf16[1,4096,2048]{2,1,0:T(8,128)(2,1)} %all-gather.3.cloned.1.call-done, bf16[2,224,2048]{2,1,0:T(8,128)(2,1)} %param.8), kind=kOutput, calls=%fused_computation.4 | convolution fusion | flops 3758096384 | bytes 21364736 | tf_op jit(solution)/shard_map/dot_general | solution.py:33
  104.1 20.5 %fusion.25 = f32[1,224,2048]{2,1,0:T(8,128)S(1)} fusion(bf16[1,4096,2048]{2,1,0:T(8,128)(2,1)} %all-gather.3.cloned.1.call-done, f32[224,4096]{1,0:T(8,128)} %fusion.4, bf16[1,224,4096]{2,1,0:T(8,128)(2,1)} %param.7, bf16[2,224,2048]{2,1,0:T(8,128)(2,1)} %param.8), kind=kOutput, calls=%fused_computation.21 | convolution fusion | flops 7526285312 | bytes 41811968 | tf_op jit(solution)/shard_map/dot_general | solution.py:40
  124.7 9.7 %fusion.30 = f32[1,224,2048]{2,1,0:T(8,128)S(1)} fusion(bf16[1,4096,2048]{2,1,0:T(8,128)(2,1)} %all-gather.3.cloned.1.call-done, f32[224,4096]{1,0:T(8,128)} %fusion.4, bf16[1,224,4096]{2,1,0:T(8,128)(2,1)} %param.7), kind=kOutput, calls=%fused_computation.22 | convolution fusion | flops 3764518912 | bytes 24117248 | tf_op jit(solution)/shard_map/dot_general | solution.py:41
  134.4 1.2 copy-done.3
  135.7 3.6 fusion.57
  139.3 0.2 all-reduce.5.cloned.1.call-start
  139.6 258.4 %all-reduce.3.cloned.1.call-done = f32[2,2048,64]{1,2,0:T(8,128)} async-done(((f32[2,2048,64]{1,2,0:T(8,128)}), f32[2,2048,64]{1,2,0:T(8,128)}) %all-reduce.3.cloned.1.call-update) | async-done | bytes 1048592 | tf_op jit(solution)/shard_map/psum | solution.py:46
  397.9 2.7 fusion.40
  400.6 0.1 copy.12
  400.7 11.7 %custom-call.7 = f32[2,64,64]{2,1,0:T(8,128)S(1)} custom-call(f32[2,64,64]{2,1,0:T(8,128)S(1)} %fusion.51), custom_call_target="Cholesky" | custom-call | tf_op jit(solution)/shard_map/jit(cholesky)/cholesky | solution.py:17
  412.5 0.1 compare_reduce_fusion
  412.6 0.1 select_bitcast_fusion
  412.7 9.8 %custom-call.8 = f32[2,1,64,64]{2,3,1,0:T(8,128)S(1)} custom-call(f32[2,1,64,64]{3,2,1,0:T(8,128)S(1)} %select_bitcast_fusion), custom_call_target="InvertDiagBlocksLowerTriangular" | custom-call | tf_op jit(solution)/shard_map/triangular_solve | solution.py:18
  422.5 2.3 fusion.38
  424.9 7.1 %fusion.56 = f32[2,224,64]{1,2,0:T(8,128)} fusion(f32[2,2048,64]{1,2,0:T(8,128)S(1)} %fusion.38, f32[1,224,2048]{2,1,0:T(8,128)} %copy-done.3, f32[1,224,2048]{2,1,0:T(8,128)S(1)} %fusion.25, f32[1,2,224,2048]{3,2,1,0:T(8,128)} %param.9), kind=kOutput, calls=%fused_computation.52 | convolution fusion | flops 706478080 | bytes 8503296 | tf_op jit(solution)/shard_map/kfd,kdr->kfr/dot_general | solution.py:48
  432.0 71.5 %all-reduce.5.cloned.1.call-done = f32[2,224,64]{1,2,0:T(8,128)} async-done(((f32[2,224,64]{1,2,0:T(8,128)}), f32[2,224,64]{1,2,0:T(8,128)}) %all-reduce.5.cloned.1.call-update) | async-done | bytes 114704 | tf_op jit(solution)/shard_map/psum | solution.py:49
  503.5 1.1 broadcast_multiply_fusion
  504.5 3.1 fusion.58
  507.6 4.8 subtract_bitcast_fusion
  512.5 1.9 subtract_convert_fusion
  (17 shorter events, 0.1 us)
Async XLA Ops:
  7.2 128.5 %copy-start = (f32[2,224,64]{1,2,0:T(8,128)S(1)}, f32[2,224,64]{1,2,0:T(8,128)}, u32[]{:S(2)}) copy-start(f32[2,224,64]{1,2,0:T(8,128)} %param.11) | copy-start | bytes 344068
  7.2 83.9 %all-gather.3.cloned.1.call-start = ((), (), s32[]{:S(2)}) async-start(), calls=%async_computation.2 | async-start | bytes 17301504 | tf_op jit(solution)/shard_map/all_gather | solution.py:31
  7.9 390.0 %all-reduce.3.cloned.1.call-start = ((), (), s32[]{:S(2)}) async-start(), calls=%async_computation | async-start | bytes 2097152 | tf_op jit(solution)/shard_map/psum | solution.py:46
  124.7 11.0 %copy-start.1 = (f32[1,2,224,2048]{3,2,1,0:T(8,128)S(1)}, f32[1,2,224,2048]{3,2,1,0:T(8,128)}, u32[]{:S(2)}) copy-start(f32[1,2,224,2048]{3,2,1,0:T(8,128)} %param.9) | copy-start | bytes 11010052
  134.4 1.3 copy-start.3
  139.3 364.2 %all-reduce.5.cloned.1.call-start = ((), (), s32[]{:S(2)}) async-start(), calls=%async_computation.1 | async-start | bytes 262144 | tf_op jit(solution)/shard_map/psum | solution.py:49
  503.5 4.2 copy-start.2
  504.5 8.0 %copy-start.4 = (f32[2,224,64]{1,2,0:T(8,128)}, f32[2,224,64]{1,2,0:T(8,128)S(1)}, u32[]{:S(2)}) copy-start(f32[2,224,64]{1,2,0:T(8,128)S(1)} %broadcast_multiply_fusion) | copy-start | bytes 344068
  507.6 4.9 copy-start.5
Sparse Core Ops, SparseCore 0:
  10.5 80.4 all-gather.2
  139.4 258.4 all-reduce.2
  432.1 71.3 all-reduce.4
where the time goes:
time: 521 us
  waiting for transfers between devices  414 us (79%)
  matrix products  62.1 us (12%)
  other arithmetic  29.6 us (6%)
  between operations  13.9 us (3%)
    psum x1, waiting for transfers between devices, per_device(): left_mean = lax.psum(left_part, ('fsdp', 'rep')) / replicas  258 us
    all_gather x1, waiting for transfers between devices, per_device(): segment = lax.all_gather(own_rows, 'fsdp', axis=0, tiled=True)  83.1 us
    psum x1, waiting for transfers between devices, per_device(): right_next = lax.psum(right_part, 'rep') / replicas  71.5 us
    dot_general x1, matrix products, per_device(): term_gate = jnp.dot(grad_gate, segment, preferred_element_type=jnp.float32)  20.5 us
    dot_general x1, matrix products, per_device(): lax.dot_general(weight[0], segment, contract_last, preferred_element_type...  13 us
    another operation x4, other arithmetic, solve_basis(): lower_factor = jnp.linalg.cholesky(gram_matrix)  11.9 us
  transfers between devices with their start and end apart: 3, of which 3 were waited for; matrix products, arithmetic and copies ran while one was open for 0% of the time, Pallas kernels for 0%

commit v1 on v0

--- a/solution.py
+++ b/solution.py
@@ -43,7 +43,7 @@
     delta = gradient + feedback[0]
     left_part = jnp.einsum("kfd,kfr->kdr", delta, right_factor, precision=highest)
     replicas = lax.axis_size("rep")
-    left_mean = lax.psum(left_part, ("fsdp", "rep")) / replicas
+    left_mean = lax.psum(lax.psum(left_part, "fsdp"), "rep") / replicas
     basis = solve_basis(left_mean, local_gram(left_mean))
     right_part = jnp.einsum("kfd,kdr->kfr", delta, basis, precision=highest)
     right_next = lax.psum(right_part, "rep") / replicas

time: 521 us -> 455 us (0.87)
  waiting for transfers between devices: 414 us -> 348 us
    psum x1 -> x2, waiting for transfers between devices: 258 us -> 193 us  [per_device(): left_mean = lax.psum(lax.psum(left_part, 'fsdp'), 'rep') / replicas]
  transfers between devices with their start and end apart: 3 -> 4, of which waited for: 3 -> 4; matrix products, arithmetic and copies ran while one was open for 0% -> 0% of each run, Pallas kernels for 0% -> 0%
where the time goes in v1:
time: 455 us
  waiting for transfers between devices  348 us (76%)
  matrix products  62.1 us (14%)
  other arithmetic  29.6 us (7%)
  between operations  13.9 us (3%)
    psum x2, waiting for transfers between devices, per_device(): left_mean = lax.psum(lax.psum(left_part, 'fsdp'), 'rep') / replicas  193 us
    all_gather x1, waiting for transfers between devices, per_device(): segment = lax.all_gather(own_rows, 'fsdp', axis=0, tiled=True)  83.1 us
    psum x1, waiting for transfers between devices, per_device(): right_next = lax.psum(right_part, 'rep') / replicas  71.1 us
    dot_general x1, matrix products, per_device(): term_gate = jnp.dot(grad_gate, segment, preferred_element_type=jnp.float32)  20.5 us
    dot_general x1, matrix products, per_device(): lax.dot_general(weight[0], segment, contract_last, preferred_element_type...  13 us
    another operation x4, other arithmetic, solve_basis(): lower_factor = jnp.linalg.cholesky(gram_matrix)  11.9 us
    another operation x3, other arithmetic, solve_basis(): lax.linalg.triangular_solve(lower_factor, factor, left_side=False, lower=...  9.92 us
    dot_general x1, matrix products, per_device(): term_up = jnp.dot(grad_up, segment, preferred_element_type=jnp.float32)  9.73 us
  transfers between devices with their start and end apart: 4, of which 4 were waited for; matrix products, arithmetic and copies ran while one was open for 0% of the time, Pallas kernels for 0%

profile of v1, /device:TPU:2, one launch (start us, length us, event | category | flops | bytes accessed | tf_op | source)
XLA Modules:
  0.0 455.2 jit_solution(7111119741998840525)
XLA Ops:
  7.2 0.7 all-gather.3.cloned.1.call-update
  8.0 83.1 %all-gather.3.cloned.1.call-done = bf16[1,4096,2048]{2,1,0:T(8,128)(2,1)} async-done(((bf16[1,128,2048]{2,1,0:T(8,128)(2,1)}), bf16[1,4096,2048]{2,1,0:T(8,128)(2,1)}) %all-gather.3.cloned.1.call-update) | async-done | bytes 16777232 | tf_op jit(solution)/shard_map/all_gather | solution.py:31
  91.1 13.0 %fusion.4 = f32[224,4096]{1,0:T(8,128)} fusion(bf16[1,4096,2048]{2,1,0:T(8,128)(2,1)} %all-gather.3.cloned.1.call-done, bf16[2,224,2048]{2,1,0:T(8,128)(2,1)} %param.8), kind=kOutput, calls=%fused_computation.4 | convolution fusion | flops 3758096384 | bytes 21364736 | tf_op jit(solution)/shard_map/dot_general | solution.py:33
  104.1 20.5 %fusion.25 = f32[1,224,2048]{2,1,0:T(8,128)S(1)} fusion(bf16[1,4096,2048]{2,1,0:T(8,128)(2,1)} %all-gather.3.cloned.1.call-done, f32[224,4096]{1,0:T(8,128)} %fusion.4, bf16[1,224,4096]{2,1,0:T(8,128)(2,1)} %param.7, bf16[2,224,2048]{2,1,0:T(8,128)(2,1)} %param.8), kind=kOutput, calls=%fused_computation.21 | convolution fusion | flops 7526285312 | bytes 41811968 | tf_op jit(solution)/shard_map/dot_general | solution.py:40
  124.7 9.7 %fusion.30 = f32[1,224,2048]{2,1,0:T(8,128)S(1)} fusion(bf16[1,4096,2048]{2,1,0:T(8,128)(2,1)} %all-gather.3.cloned.1.call-done, f32[224,4096]{1,0:T(8,128)} %fusion.4, bf16[1,224,4096]{2,1,0:T(8,128)(2,1)} %param.7), kind=kOutput, calls=%fused_computation.22 | convolution fusion | flops 3764518912 | bytes 24117248 | tf_op jit(solution)/shard_map/dot_general | solution.py:41
  134.4 1.2 copy-done.3
  135.7 3.6 fusion.57
  139.3 0.0 all-reduce.6.cloned.1.call-start
  139.3 114.6 %all-reduce.4.cloned.1.call-done = f32[2,2048,64]{1,2,0:T(8,128)} async-done(((f32[2,2048,64]{1,2,0:T(8,128)}), f32[2,2048,64]{1,2,0:T(8,128)}) %all-reduce.4.cloned.1.call-update) | async-done | bytes 1048592 | tf_op jit(solution)/shard_map/psum | solution.py:46
  253.9 0.2 all-reduce.8.cloned.1.call-start
  254.2 78.4 %all-reduce.6.cloned.1.call-done = f32[2,2048,64]{1,2,0:T(8,128)} async-done(((f32[2,2048,64]{1,2,0:T(8,128)}), f32[2,2048,64]{1,2,0:T(8,128)}) %all-reduce.6.cloned.1.call-update) | async-done | bytes 1048592 | tf_op jit(solution)/shard_map/psum | solution.py:46
  332.6 2.7 fusion.40
  335.3 0.1 copy.12
  335.4 11.7 %custom-call.7 = f32[2,64,64]{2,1,0:T(8,128)S(1)} custom-call(f32[2,64,64]{2,1,0:T(8,128)S(1)} %fusion.51), custom_call_target="Cholesky" | custom-call | tf_op jit(solution)/shard_map/jit(cholesky)/cholesky | solution.py:17
  347.2 0.1 compare_reduce_fusion
  347.3 0.1 select_bitcast_fusion
  347.4 9.8 %custom-call.8 = f32[2,1,64,64]{2,3,1,0:T(8,128)S(1)} custom-call(f32[2,1,64,64]{3,2,1,0:T(8,128)S(1)} %select_bitcast_fusion), custom_call_target="InvertDiagBlocksLowerTriangular" | custom-call | tf_op jit(solution)/shard_map/triangular_solve | solution.py:18
  357.2 2.3 fusion.38
  359.6 7.1 %fusion.56 = f32[2,224,64]{1,2,0:T(8,128)} fusion(f32[2,2048,64]{1,2,0:T(8,128)S(1)} %fusion.38, f32[1,224,2048]{2,1,0:T(8,128)} %copy-done.3, f32[1,224,2048]{2,1,0:T(8,128)S(1)} %fusion.25, f32[1,2,224,2048]{3,2,1,0:T(8,128)} %param.9), kind=kOutput, calls=%fused_computation.52 | convolution fusion | flops 706478080 | bytes 8503296 | tf_op jit(solution)/shard_map/kfd,kdr->kfr/dot_general | solution.py:48
  366.7 71.1 %all-reduce.8.cloned.1.call-done = f32[2,224,64]{1,2,0:T(8,128)} async-done(((f32[2,224,64]{1,2,0:T(8,128)}), f32[2,224,64]{1,2,0:T(8,128)}) %all-reduce.8.cloned.1.call-update) | async-done | bytes 114704 | tf_op jit(solution)/shard_map/psum | solution.py:49
  437.8 1.1 broadcast_multiply_fusion
  438.9 3.1 fusion.58
  442.0 4.8 %subtract_bitcast_fusion = f32[1,2,224,2048]{3,2,1,0:T(8,128)} fusion(f32[2,224,2048]{2,1,0:T(8,128)S(1)} %fusion.58, f32[1,2,224,2048]{3,2,1,0:T(8,128)S(1)} %copy-done.2, f32[1,224,2048]{2,1,0:T(8,128)} %copy-done.3, f32[1,224,2048]{2,1,0:T(8,128)S(1)} %fusion.25), kind=kLoop, calls=%fused_computation.15 | loop fusion | flops 2752512 | bytes 14680064 | tf_op jit(solution)/shard_map/broadcast_in_dim | solution.py:51
  446.8 1.9 subtract_convert_fusion
  (20 shorter events, 0.2 us)
Async XLA Ops:
  7.2 128.5 %copy-start = (f32[2,224,64]{1,2,0:T(8,128)S(1)}, f32[2,224,64]{1,2,0:T(8,128)}, u32[]{:S(2)}) copy-start(f32[2,224,64]{1,2,0:T(8,128)} %param.11) | copy-start | bytes 344068
  7.2 83.9 %all-gather.3.cloned.1.call-start = ((), (), s32[]{:S(2)}) async-start(), calls=%async_computation.3 | async-start | bytes 17301504 | tf_op jit(solution)/shard_map/all_gather | solution.py:31
  7.9 246.0 %all-reduce.4.cloned.1.call-start = ((), (), s32[]{:S(2)}) async-start(), calls=%async_computation | async-start | bytes 2097152 | tf_op jit(solution)/shard_map/psum | solution.py:46
  124.7 11.0 %copy-start.1 = (f32[1,2,224,2048]{3,2,1,0:T(8,128)S(1)}, f32[1,2,224,2048]{3,2,1,0:T(8,128)}, u32[]{:S(2)}) copy-start(f32[1,2,224,2048]{3,2,1,0:T(8,128)} %param.9) | copy-start | bytes 11010052
  134.4 1.3 copy-start.3
  139.3 193.3 %all-reduce.6.cloned.1.call-start = ((), (), s32[]{:S(2)}) async-start(), calls=%async_computation.1 | async-start | bytes 2097152 | tf_op jit(solution)/shard_map/psum | solution.py:46
  253.9 183.9 %all-reduce.8.cloned.1.call-start = ((), (), s32[]{:S(2)}) async-start(), calls=%async_computation.2 | async-start | bytes 262144 | tf_op jit(solution)/shard_map/psum | solution.py:49
  437.8 4.2 copy-start.2
  438.9 8.0 %copy-start.4 = (f32[2,224,64]{1,2,0:T(8,128)}, f32[2,224,64]{1,2,0:T(8,128)S(1)}, u32[]{:S(2)}) copy-start(f32[2,224,64]{1,2,0:T(8,128)S(1)} %broadcast_multiply_fusion) | copy-start | bytes 344068
  442.0 4.9 %copy-start.5 = (f32[2,224,256]{2,1,0:T(8,128)S(1)}, f32[2,224,256]{2,1,0:T(8,128)}, u32[]{:S(2)}) copy-start(f32[2,224,256]{2,1,0:T(8,128)} %param.10) | copy-start | bytes 1376260
Sparse Core Ops, SparseCore 0:
  10.5 80.4 all-gather.2
  139.4 114.4 all-reduce.3
  256.3 76.3 all-reduce.5
  366.8 70.9 all-reduce.7
